TPU v7x, 32 devices: a whole 2x2x4 slice. The times are simulated.
32 devices in a mesh: wide: 8 (over y, x, core), narrow: 4 (over z).
Axes of the slice: x: 2, y: 2, z: 4, core: 2. Of those that a mesh axis runs over, the one named last changes fastest.
Arguments:
- batch_index: int32 [256], P('narrow'), may hold values from 0 to 255
- train_features: float32 [1024, 1024], P('narrow'), may hold values from -6 to 6
- train_labels: float32 [1024, 1000], P('narrow'), may hold values from -12 to 12
- centers: float32 [8192, 1024], P(('wide', 'narrow')), may hold values from -6 to 6
- weights: float32 [8192, 1000], P(('wide', 'narrow')), may hold values from -6 to 6
Outputs:
- new_weights: float32 [8192, 1000], P(('wide', 'narrow'))
- residual: float32 [256, 1000], P('narrow')
Inputs may be any that keep to these rules, and one draw needn't show every extreme that they name: `batch_index`: entry i names a row of the training shard held by narrow index i // 64.
All inputs are finite; a program needn't handle non-finite values.
Results may differ from a plain program's by a relative error of at most 0.0001.
Values sent between devices are 32-bit elements; how exact they have to be, the bound alone decides.
A program may use at most 64 MiB of HBM per device.

v0:
```python
import math
import jax
import jax.numpy as jnp
from jax import lax
from jax.sharding import PartitionSpec as P

step_size = 1.0


def per_device(batch_index, train_features, train_labels, centers, weights):
    rows = jnp.take(train_features, batch_index, axis=0)
    targets = jnp.take(train_labels, batch_index, axis=0)
    features = centers.shape[1]
    center_sq = jnp.sum(centers * centers, axis=1)
    count = centers.shape[0] * lax.axis_size("wide") * lax.axis_size("narrow")
    scale = 1.0 / math.sqrt(count)
    piece = lax.all_gather(rows, "narrow", axis=0, tiled=True)
    inner = jnp.dot(
        piece, centers.T, precision=lax.Precision.HIGHEST, preferred_element_type=jnp.float32
    )
    piece_sq = jnp.sum(piece * piece, axis=1)
    kernel = jnp.exp(
        (2.0 * features - piece_sq[:, None] - center_sq[None, :] + 2.0 * inner) / 128.0
    )
    batch = kernel.shape[0]
    kern_rows = kernel
    local = lax.psum_scatter(
        jnp.dot(
            kern_rows, weights, precision=lax.Precision.HIGHEST, preferred_element_type=jnp.float32
        ),
        "narrow",
        scatter_dimension=0,
        tiled=True,
    )
    predicted = lax.psum(local, "wide") * scale
    residual = predicted - targets
    kern_rows = kernel
    delta = lax.dot_general(
        kern_rows,
        lax.all_gather(residual, "narrow", axis=0, tiled=True),
        (((0,), (0,)), ((), ())),
        precision=lax.Precision.HIGHEST,
        preferred_element_type=jnp.float32,
    )
    new_weights = weights - step_size / batch * delta
    return (new_weights, residual)


def solution(mesh):
    in_specs = (
        P("narrow"),
        P("narrow", None),
        P("narrow", None),
        P(("wide", "narrow"), None),
        P(("wide", "narrow"), None),
    )
    out_specs = (P(("wide", "narrow"), None), P("narrow", None))
    return jax.shard_map(
        per_device, mesh=mesh, in_specs=in_specs, out_specs=out_specs, check_vma=False
    )
```

profile of v0, /device:TPU:0, one launch (start us, length us, event | category | flops | bytes accessed | tf_op | source)
XLA Modules:
  0.0 160.9 jit_solution(7561517133553205740)
XLA Ops:
  7.2 0.0 all-gather.2.cloned.1.call-start
  7.2 0.7 compare_and_fusion
  8.0 0.4 copy-done
  8.4 0.7 gather_fusion
  9.1 0.8 broadcast_select_fusion
  9.9 0.0 all-gather.2.cloned.1.call-update
  9.9 0.0 reduce-scatter.2.cloned.1.call-start
  10.0 0.1 multiply_reduce_fusion
  10.1 30.7 %all-gather.2.cloned.1.call-done = f32[256,1024]{1,0:T(8,128)} async-done(((f32[64,1024]{1,0:T(8,128)}), f32[256,1024]{1,0:T(8,128)}) %all-gather.2.cloned.1.call-update) | async-done | bytes 1048592 | tf_op jit(solution)/shard_map/all_gather | solution.py:17
  40.9 1.5 multiply_reduce_fusion.1
  42.4 0.1 copy-done.2
  42.4 1.1 fusion.3
  43.5 0.1 copy-done.3
  43.6 2.0 %fusion.4 = f32[256,1000]{1,0:T(8,128)} fusion(f32[256,256]{1,0:T(8,128)S(1)} %fusion.3, f32[256,1000]{0,1:T(8,128)S(1)} %copy-done.3), kind=kOutput, calls=%fused_computation.16 | convolution fusion | flops 786432000 | bytes 2310144 | tf_op jit(solution)/shard_map/dot_general | solution.py:28
  45.7 0.0 reduce-scatter.2.cloned.1.call-update
  45.7 0.0 all-reduce.2.cloned.1.call-start
  45.7 26.8 %reduce-scatter.2.cloned.1.call-done = f32[64,1000]{1,0:T(8,128)} async-done(((f32[256,1000]{1,0:T(8,128)}), f32[64,1000]{1,0:T(8,128)}) %reduce-scatter.2.cloned.1.call-update) | async-done | bytes 256016 | tf_op jit(solution)/shard_map/reduce_scatter | solution.py:27
  72.5 0.0 all-reduce.2.cloned.1.call-update
  72.5 1.5 copy.7
  74.1 1.4 gather_fusion.1
  75.5 52.5 %all-reduce.2.cloned.1.call-done = f32[64,1000]{1,0:T(8,128)} async-done(((f32[64,1000]{1,0:T(8,128)}), f32[64,1000]{1,0:T(8,128)}) %all-reduce.2.cloned.1.call-update) | async-done | bytes 256016 | tf_op jit(solution)/shard_map/psum | solution.py:35
  128.0 1.1 select_subtract_fusion
  129.1 22.5 %all_gather.7 = f32[256,1000]{1,0:T(8,128)S(1)} all-gather(f32[64,1000]{1,0:T(8,128)S(1)} %select_subtract_fusion), channel_id=1, replica_groups=mesh['wide'=8,'narrow'=4] {'narrow'}, dimensions={0}, use_global_device_ids=true | all-gather | bytes 1280000 | tf_op jit(solution)/shard_map/all_gather | solution.py:40
  151.6 2.8 %fusion = f32[256,1000]{0,1:T(8,128)} fusion(f32[256,1000]{0,1:T(8,128)S(1)} %copy-done.3, f32[256,256]{1,0:T(8,128)S(1)} %fusion.3, f32[256,1000]{1,0:T(8,128)S(1)} %all_gather.7), kind=kOutput, calls=%fused_computation.3 | convolution fusion | flops 786944000 | bytes 3334144 | tf_op jit(solution)/shard_map/dot_general | solution.py:38
  (12 shorter events, 0.0 us)
Async XLA Ops:
  7.2 1.3 copy-start
  7.2 0.8 copy-start.5
  7.2 33.7 %all-gather.2.cloned.1.call-start = ((), (), s32[]{:S(2)}) async-start(), calls=%async_computation.1 | async-start | bytes 1310720 | tf_op jit(solution)/shard_map/all_gather | solution.py:17
  8.4 1.6 copy-start.1
  9.9 62.6 %reduce-scatter.2.cloned.1.call-start = ((), (), s32[]{:S(2)}) async-start(), calls=%async_computation.2 | async-start | bytes 1310720 | tf_op jit(solution)/shard_map/reduce_scatter | solution.py:27
  40.9 1.5 copy-start.2
  42.4 1.2 copy-start.3
  45.7 82.3 %all-reduce.2.cloned.1.call-start = ((), (), s32[]{:S(2)}) async-start(), calls=%async_computation.3 | async-start | bytes 524288 | tf_op jit(solution)/shard_map/psum | solution.py:35
  129.1 22.5 %copy-start.4 = (f32[64,1000]{1,0:T(8,128)}, f32[64,1000]{1,0:T(8,128)S(1)}, u32[]{:S(2)}) copy-start(f32[64,1000]{1,0:T(8,128)S(1)} %select_subtract_fusion) | copy-start | bytes 768004
Sparse Core Ops, SparseCore 0:
  10.1 30.6 all-gather.1
  45.8 26.6 reduce-scatter.1
  75.6 52.3 all-reduce.1
where the time goes:
time: 161 us
  waiting for transfers between devices  110 us (68%)
  blocking collectives  22.5 us (14%)
  between operations  13.8 us (9%)
  matrix products  5.91 us (4%)
  other arithmetic  4.28 us (3%)
  local copies, waits for them, and re-layouts  4.26 us (3%)
    psum x1, waiting for transfers between devices, per_device(): predicted = lax.psum(local, 'wide') * scale  52.5 us
    all_gather x1, waiting for transfers between devices, per_device(): piece = lax.all_gather(rows, 'narrow', axis=0, tiled=True)  30.7 us
    reduce_scatter x1, waiting for transfers between devices, per_device(): lax.psum_scatter(jnp.dot(kern_rows, weights, precision=lax.Precision.HIGH...  26.8 us
    all_gather x1, blocking collectives, per_device(): lax.all_gather(residual, 'narrow', axis=0, tiled=True)  22.5 us
  transfers between devices with their start and end apart: 3, of which 3 were waited for; matrix products, arithmetic and copies ran while one was open for 2% of the time, Pallas kernels for 0%

commit v1 on v0

--- a/solution.py
+++ b/solution.py
@@ -5,6 +5,11 @@
 from jax.sharding import PartitionSpec as P
 
 step_size = 1.0
+
+
+def add_all(shard, axis):
+    blocks = lax.all_gather(shard, axis)
+    return jnp.sum(blocks, axis=0)
 
 
 def per_device(batch_index, train_features, train_labels, centers, weights):
@@ -32,7 +37,7 @@
         scatter_dimension=0,
         tiled=True,
     )
-    predicted = lax.psum(local, "wide") * scale
+    predicted = add_all(local, "wide") * scale
     residual = predicted - targets
     kern_rows = kernel
     delta = lax.dot_general(

time: 161 us -> 136 us (0.84)
  waiting for transfers between devices: 110 us -> 82.7 us
    psum x1 -> x0, waiting for transfers between devices: 52.5 us -> none  [per_device(): predicted = lax.psum(local, 'wide') * scale]
    all_gather x0 -> x1, waiting for transfers between devices: none -> 25.2 us  [add_all(): blocks = lax.all_gather(shard, axis)]
    reduce_sum x0 -> x1, other arithmetic: none -> 1.76 us  [add_all(): return jnp.sum(blocks, axis=0)]
where the time goes in v1:
time: 136 us
  waiting for transfers between devices  82.7 us (61%)
  blocking collectives  22.5 us (17%)
  between operations  13.8 us (10%)
  matrix products  7.13 us (5%)
  other arithmetic  5.64 us (4%)
  local copies, waits for them, and re-layouts  3.63 us (3%)
    all_gather x1, waiting for transfers between devices, per_device(): piece = lax.all_gather(rows, 'narrow', axis=0, tiled=True)  30.6 us
    reduce_scatter x1, waiting for transfers between devices, per_device(): lax.psum_scatter(jnp.dot(kern_rows, weights, precision=lax.Precision.HIGH...  26.8 us
    all_gather x1, waiting for transfers between devices, add_all(): blocks = lax.all_gather(shard, axis)  25.2 us
    all_gather x1, blocking collectives, per_device(): lax.all_gather(residual, 'narrow', axis=0, tiled=True)  22.5 us
    dot_general x1, matrix products, per_device(): lax.dot_general(kern_rows, lax.all_gather(residual, 'narrow', axis=0, til...  2.82 us
  transfers between devices with their start and end apart: 3, of which 3 were waited for; matrix products, arithmetic and copies ran while one was open for 2% of the time, Pallas kernels for 0%

profile of v1, /device:TPU:0, one launch (start us, length us, event | category | flops | bytes accessed | tf_op | source)
XLA Modules:
  0.0 135.6 jit_solution(15014058737612504367)
XLA Ops:
  7.2 0.0 copy-start
  7.2 0.0 all-gather.4.cloned.1.call-start
  7.2 0.8 compare_and_fusion
  8.0 0.7 compare_select_fusion
  8.7 0.7 gather_fusion
  9.4 0.8 broadcast_select_fusion
  10.2 0.0 all-gather.4.cloned.1.call-update
  10.2 0.0 reduce-scatter.2.cloned.1.call-start
  10.3 0.1 multiply_reduce_fusion
  10.4 30.6 %all-gather.4.cloned.1.call-done = f32[256,1024]{1,0:T(8,128)} async-done(((f32[64,1024]{1,0:T(8,128)}), f32[256,1024]{1,0:T(8,128)}) %all-gather.4.cloned.1.call-update) | async-done | bytes 1048592 | tf_op jit(solution)/shard_map/all_gather | solution.py:22
  41.1 1.4 %multiply_reduce_fusion.1 = f32[256]{0:T(256)S(1)} fusion(f32[256,1024]{1,0:T(8,128)} %all-gather.4.cloned.1.call-done), kind=kLoop, calls=%fused_computation.9 | loop fusion | flops 524032 | bytes 1049600 | tf_op jit(solution)/shard_map/reduce_sum | solution.py:26
  42.4 2.3 %fusion.3 = f32[256,256]{1,0:T(8,128)S(1)} fusion(f32[256,1024]{1,0:T(8,128)} %all-gather.4.cloned.1.call-done, f32[256,1024]{1,0:T(8,128)S(1)} %copy-done.1, f32[256]{0:T(256)S(1)} %multiply_reduce_fusion, f32[256]{0:T(256)S(1)} %broadcast_subtract_fusion), kind=kOutput, calls=%fused_computation.7 | convolution fusion | flops 805568512 | bytes 2361344 | tf_op jit(solution)/shard_map/dot_general | solution.py:23
  44.7 2.0 %fusion.4 = f32[256,1000]{1,0:T(8,128)} fusion(f32[256,256]{1,0:T(8,128)S(1)} %fusion.3, f32[256,1000]{0,1:T(8,128)S(1)} %copy-done.2), kind=kOutput, calls=%fused_computation.16 | convolution fusion | flops 786432000 | bytes 2310144 | tf_op jit(solution)/shard_map/dot_general | solution.py:33
  46.8 0.0 reduce-scatter.2.cloned.1.call-update
  46.8 0.0 all-gather.6.cloned.1.call-start
  46.9 26.8 %reduce-scatter.2.cloned.1.call-done = f32[64,1000]{1,0:T(8,128)} async-done(((f32[256,1000]{1,0:T(8,128)}), f32[64,1000]{1,0:T(8,128)}) %reduce-scatter.2.cloned.1.call-update) | async-done | bytes 256016 | tf_op jit(solution)/shard_map/reduce_scatter | solution.py:32
  73.6 0.0 all-gather.6.cloned.1.call-update
  73.7 1.5 %copy.7 = f32[256,1000]{1,0:T(8,128)S(1)} copy(f32[256,1000]{0,1:T(8,128)} %param.7) | data formatting | bytes 2048000 | tf_op args[2]
  75.2 1.4 %gather_fusion.1 = f32[64,1000]{1,0:T(8,128)} fusion(f32[256,1000]{1,0:T(8,128)S(1)} %copy.7, s32[1024]{0:T(1024)S(1)} %pad_clamp_fusion), kind=kCustom, calls=%fused_computation.1 | custom fusion | bytes 512256 | tf_op jit(solution)/shard_map/jit(_take)/gather | solution.py:17
  76.6 25.2 %all-gather.6.cloned.1.call-done = f32[512,1000]{1,0:T(8,128)} async-done(((f32[64,1000]{1,0:T(8,128)}), f32[512,1000]{1,0:T(8,128)}) %all-gather.6.cloned.1.call-update) | async-done | bytes 2048016 | tf_op jit(solution)/shard_map/all_gather | solution.py:11
  101.8 1.8 %reduce_sum.29 = f32[64,1000]{1,0:T(8,128)S(1)} reduce(f32[8,64,1000]{2,1,0:T(8,128)} %bitcast.7, f32[]{:T(128)} %constant.36.clone.1), dimensions={0}, to_apply=%region_3.4 | reduce | flops 448000 | bytes 2304004 | tf_op jit(solution)/shard_map/reduce_sum | solution.py:12
  103.6 0.1 select_subtract_fusion
  103.7 22.5 %all_gather.15 = f32[256,1000]{1,0:T(8,128)S(1)} all-gather(f32[64,1000]{1,0:T(8,128)S(1)} %select_subtract_fusion), channel_id=1, replica_groups=mesh['wide'=8,'narrow'=4] {'narrow'}, dimensions={0}, use_global_device_ids=true | all-gather | bytes 1280000 | tf_op jit(solution)/shard_map/all_gather | solution.py:45
  126.2 2.8 %fusion = f32[256,1000]{0,1:T(8,128)} fusion(f32[256,1000]{0,1:T(8,128)S(1)} %copy-done.2, f32[256,256]{1,0:T(8,128)S(1)} %fusion.3, f32[256,1000]{1,0:T(8,128)S(1)} %all_gather.15), kind=kOutput, calls=%fused_computation.3 | convolution fusion | flops 786944000 | bytes 3334144 | tf_op jit(solution)/shard_map/dot_general | solution.py:43
  (11 shorter events, 0.0 us)
Async XLA Ops:
  7.2 1.5 %copy-start = (f32[256,1024]{1,0:T(8,128)S(1)}, f32[256,1024]{1,0:T(8,128)}, u32[]{:S(2)}) copy-start(f32[256,1024]{1,0:T(8,128)} %param.6) | copy-start | bytes 3145732
  7.2 3.1 %copy-start.1 = (f32[256,1024]{1,0:T(8,128)S(1)}, f32[256,1024]{1,0:T(8,128)}, u32[]{:S(2)}) copy-start(f32[256,1024]{1,0:T(8,128)} %param.8) | copy-start | bytes 3145732
  7.2 33.9 %all-gather.4.cloned.1.call-start = ((), (), s32[]{:S(2)}) async-start(), calls=%async_computation.1 | async-start | bytes 1310720 | tf_op jit(solution)/shard_map/all_gather | solution.py:22
  10.2 34.5 %copy-start.2 = (f32[256,1000]{0,1:T(8,128)S(1)}, f32[256,1000]{0,1:T(8,128)}, u32[]{:S(2)}) copy-start(f32[256,1000]{0,1:T(8,128)} %param.9) | copy-start | bytes 3072004
  10.2 63.4 %reduce-scatter.2.cloned.1.call-start = ((), (), s32[]{:S(2)}) async-start(), calls=%async_computation.2 | async-start | bytes 1310720 | tf_op jit(solution)/shard_map/reduce_scatter | solution.py:32
  46.8 55.0 %all-gather.6.cloned.1.call-start = ((), (), s32[]{:S(2)}) async-start(), calls=%async_computation.3 | async-start | bytes 2359296 | tf_op jit(solution)/shard_map/all_gather | solution.py:11
  76.6 27.0 %copy-start.4 = (f32[64,1000]{1,0:T(8,128)S(1)}, f32[64,1000]{1,0:T(8,128)}, u32[]{:S(2)}) copy-start(f32[64,1000]{1,0:T(8,128)} %gather_fusion.1) | copy-start | bytes 768004
  103.7 25.4 %copy-start.3 = (f32[64,1000]{1,0:T(8,128)}, f32[64,1000]{1,0:T(8,128)S(1)}, u32[]{:S(2)}) copy-start(f32[64,1000]{1,0:T(8,128)S(1)} %select_subtract_fusion) | copy-start | bytes 768004
Sparse Core Ops, SparseCore 0:
  10.3 30.6 all-gather.3
  46.9 26.6 reduce-scatter.1
  75.5 26.2 all-gather.5
